TPU v7x, 512 devices: a whole 4x8x8 slice. The times are simulated.
512 devices in a mesh: bin: 64 (over z, x, y_hi), grp: 8 (over y_lo, core).
Axes of the slice: x: 4, y: 8 (y_hi: 2, y_lo: 4; y = y_hi * 4 + y_lo), z: 8, core: 2. Of those that a mesh axis runs over, the one named last changes fastest.
Arguments:
- record: bfloat16 [8, 256, 8704], P('grp', 'bin'), may hold values from -60 to 60
- ref_index: int32 [8, 16], P('grp'), may hold values from 0 to 255, as said below
- offsets: int32 [16], replicated, may hold values from 0 to 7680, as said below
Outputs:
- transfer: bfloat16 [512, 2048, 256], P('bin', 'grp')
Inputs may be any that keep to these rules, and one draw needn't show every extreme that they name: `ref_index`: each row lists 16 different channels of its group; every row holds 0 and 255. `offsets`: starts rise; the first is 0, the last is 7680, and neighbours lie 512 // 2 to 768 apart.
All inputs are finite; a program needn't handle non-finite values.
Results may differ from a plain program's by a relative error of at most 0.0095.
Values may be sent and summed in bfloat16 or wider, within the bound.
A program may use at most 64 MiB of HBM per device.

v0:
```python
import math

import jax
import jax.numpy as jnp
from jax import lax
from jax.sharding import PartitionSpec as P

L = 1024
NB = 512


ridge_weight = 0.5


def make_table(seg_len, bins):
    sample_num = lax.iota(jnp.int32, seg_len)[:, None]
    bin_num = lax.iota(jnp.int32, bins)[None, :]
    angles = (sample_num * bin_num % seg_len).astype(jnp.float32) * (2.0 * math.pi / seg_len)
    hann_window = 0.5 - 0.5 * jnp.cos(sample_num.astype(jnp.float32) * (2.0 * math.pi / seg_len))
    return jnp.concatenate(
        [hann_window * jnp.cos(angles), -(hann_window * jnp.sin(angles))], axis=1
    ).astype(jnp.bfloat16)


def transform(chan_rows, starts, dft_table, bin_devices):
    seg_len = dft_table.shape[0]
    pieces = jax.vmap(lambda start_at: lax.dynamic_slice_in_dim(chan_rows, start_at, seg_len, 1))(
        starts
    )
    spectra = jnp.einsum(
        "scn,nk->ksc", pieces, dft_table, preferred_element_type=jnp.float32
    ).astype(jnp.bfloat16)
    bin_total = dft_table.shape[1] // 2
    return spectra.reshape(
        2, bin_devices, bin_total // bin_devices, starts.shape[0], chan_rows.shape[0]
    )


def local(record, ref_index, offsets):
    chan_rows = record[0]
    dft_table = make_table(L, NB)
    bin_devices = lax.axis_size("bin")
    spectra = transform(chan_rows, offsets, dft_table, bin_devices)
    channels = lax.all_to_all(spectra, "bin", split_axis=1, concat_axis=4, tiled=True)[:, 0]
    local_refs = jnp.take(channels, ref_index[0], axis=3)
    references = lax.all_gather(local_refs, "grp", axis=3, tiled=True)
    ref_real = references[0]
    ref_imag = references[1]
    ref_blocks = jnp.stack(
        [
            jnp.concatenate([ref_real, -ref_imag], axis=-1),
            jnp.concatenate([ref_imag, ref_real], axis=-1),
        ]
    )
    bins_here = channels.shape[1]
    group_size = math.gcd(bins_here, 4)
    group_count = bins_here // group_size
    real_order = ref_blocks.shape[-1]

    def solve_group(group_index):
        first_bin = group_index * group_size
        ref_group = lax.dynamic_slice_in_dim(ref_blocks, first_bin, group_size, 1)
        chan_group = lax.dynamic_slice_in_dim(channels, first_bin, group_size, 1)
        cross_part = jnp.einsum(
            "pfsr,pfsc->frc", ref_group, chan_group, preferred_element_type=jnp.float32
        )
        auto_part = jnp.einsum(
            "pfsr,pfsq->frq", ref_group, ref_group, preferred_element_type=jnp.float32
        )
        ridge_term = ridge_weight * jnp.trace(auto_part, axis1=1, axis2=2) / real_order
        factor = jnp.linalg.cholesky(
            auto_part + ridge_term[:, None, None] * jnp.eye(real_order, dtype=jnp.float32)
        )
        transfer_t = jax.scipy.linalg.cho_solve((factor, True), cross_part)
        return jnp.swapaxes(transfer_t, 1, 2).astype(jnp.bfloat16)

    results = lax.map(solve_group, jnp.arange(group_count))
    return results.reshape(bins_here, results.shape[2], results.shape[3])


def solution(mesh):
    placed = (P("grp", "bin", None), P("grp", None), P())
    return jax.shard_map(
        local, mesh=mesh, in_specs=placed, out_specs=P("bin", "grp", None), check_vma=False
    )
```

profile of v0, /device:TPU:1, one launch (start us, length us, event | category | flops | bytes accessed | tf_op | source)
XLA Modules:
  0.0 550.2 jit_solution(7552281096765540275)
XLA Ops:
  0.1 8.9 %multiply_convert_fusion = (bf16[1024,512]{1,0:T(8,128)(2,1)S(1)}, bf16[1024,512]{1,0:T(8,128)(2,1)S(1)}) fusion(f32[1024]{0:T(1024)S(1)} %multiply_subtract_fusion), kind=kLoop, calls=%fused_computation.58 | loop fusion | flops 9961472 | bytes 2101248 | tf_op jit(solution)/shard_map/convert.2
  9.0 32.3 %while.17 = (s32[]{:T(128)}, bf16[4,8704]{1,0:T(4,128)(2,1)}, s32[16,2]{0,1:T(2,128)S(1)}, bf16[16,4,1024]{2,1,0:T(4,128)(2,1)S(1)}, s32[]{:T(128)}) while((s32[]{:T(128)}, bf16[4,8704]{1,0:T(4,128)(2,1)}, s32[16,2]{0,1:T(2,128)S(1)}, bf16[16,4,1024]{2,1,0:T(4,128)(2,1)S(1)}, s32[]{:T(128)}) %tuple.87), condition=%wide.while_cond.1, body=%wide.while_body.1.sunk | while | flops 2 | bytes 16481 | solution.py:27
  9.6 1.4 bitcast_dynamic-update-slice_fusion.4
  11.6 1.4 bitcast_dynamic-update-slice_fusion.4
  13.6 1.4 bitcast_dynamic-update-slice_fusion.4
  15.7 1.4 bitcast_dynamic-update-slice_fusion.4
  17.7 1.4 bitcast_dynamic-update-slice_fusion.4
  19.7 1.4 bitcast_dynamic-update-slice_fusion.4
  21.7 1.4 bitcast_dynamic-update-slice_fusion.4
  23.7 1.4 bitcast_dynamic-update-slice_fusion.4
  25.7 1.4 bitcast_dynamic-update-slice_fusion.4
  27.7 1.4 bitcast_dynamic-update-slice_fusion.4
  29.8 1.4 bitcast_dynamic-update-slice_fusion.4
  31.8 1.4 bitcast_dynamic-update-slice_fusion.4
  33.8 1.4 bitcast_dynamic-update-slice_fusion.4
  35.8 1.4 bitcast_dynamic-update-slice_fusion.4
  37.8 1.4 bitcast_dynamic-update-slice_fusion.4
  39.8 1.4 bitcast_dynamic-update-slice_fusion.4
  42.5 1.8 reshape.166
  44.3 19.6 %all-to-all-start = ((bf16[64,2,512]{2,1,0:T(2,128)(2,1)}), bf16[64,2,512]{2,1,0:T(2,128)(2,1)S(1)}, u32[]{:S(2)}, u32[]{:S(2)}) async-start(bf16[64,2,512]{2,1,0:T(2,128)(2,1)} %reshape.166), calls=%async_computation | async-start | bytes 262144 | tf_op jit(solution)/shard_map/all_to_all | solution.py:44
  63.9 13.6 %all-to-all-done = bf16[64,2,512]{2,1,0:T(2,128)(2,1)S(1)} async-done(((bf16[64,2,512]{2,1,0:T(2,128)(2,1)}), bf16[64,2,512]{2,1,0:T(2,128)(2,1)S(1)}, u32[]{:S(2)}, u32[]{:S(2)}) %all-to-all-start) | async-done | bytes 131104 | tf_op jit(solution)/shard_map/all_to_all | solution.py:44
  77.5 0.7 reshape.167
  78.6 0.6 gather_fusion
  79.3 16.7 %all_gather.3 = bf16[2,8,16,128]{2,1,0,3:T(8,128)(2,1)S(1)} all-gather(bf16[2,8,16,16]{2,1,0,3:T(8,128)(2,1)S(1)} %select_bitcast_fusion.1), channel_id=1, replica_groups=mesh['bin'=64,'grp'=8] {'grp'}, dimensions={3}, use_global_device_ids=true | all-gather | bytes 73728 | tf_op jit(solution)/shard_map/all_gather | solution.py:46
  96.6 0.8 copy.60
  97.5 452.7 %while.16 = (s32[]{:T(128)}, bf16[2,4,256,256]{3,2,1,0:T(8,128)(2,1)}, s32[2]{0:T(128)S(1)}, bf16[2,8,16,256]{3,2,1,0:T(8,128)(2,1)S(1)}, bf16[2,8,16,256]{3,2,0...) while((s32[]{:T(128)}, ...), condition=%wide.region_6.7_spmd, body=%wide.region_0.6_spmd.sunk | while | flops 1448117248 | bytes 37234176 | solution.py:77
  97.6 0.6 dynamic_slice.33
  100.1 46.9 %custom-call.42 = f32[4,128,128]{2,1,0:T(8,128)S(1)} custom-call(f32[4,128,128]{2,1,0:T(8,128)S(1)} %cholesky.172), custom_call_target="Cholesky" | custom-call | tf_op jit(solution)/shard_map/while/body/eval_jaxpr/jit(cholesky)/cholesky | solution.py:71
  147.1 39.3 %custom-call.43 = f32[4,1,128,128]{2,3,1,0:T(8,128)S(1)} custom-call(f32[4,1,128,128]{3,2,1,0:T(8,128)S(1)} %select_bitcast_fusion.3), custom_call_target="InvertDiagBlocksLowerTriangular" | custom-call | tf_op jit(solution)/shard_map/while/body/eval_jaxpr/jit(cholesky)/cholesky | solution.py:71
  186.9 0.7 convolution_subtract_fusion.6
  187.5 46.9 %custom-call.44 = f32[4,128,128]{2,1,0:T(8,128)S(1)} custom-call(f32[4,128,128]{2,1,0:T(8,128)S(1)} %convolution_subtract_fusion.6), custom_call_target="Cholesky" | custom-call | tf_op jit(solution)/shard_map/while/body/eval_jaxpr/jit(cholesky)/cholesky | solution.py:71
  235.1 3.9 while.18
  235.1 0.6 fusion.74
  235.7 1.3 bitcast_dynamic-update-slice_fusion.5
  237.0 0.6 fusion.74
  237.7 1.3 bitcast_dynamic-update-slice_fusion.5
  239.0 78.6 %custom-call.46 = f32[4,2,128,128]{2,3,1,0:T(8,128)S(1)} custom-call(f32[4,2,128,128]{3,2,1,0:T(8,128)S(1)} %bitcast.144), custom_call_target="InvertDiagBlocksLowerTriangular" | custom-call | tf_op jit(solution)/shard_map/while/body/eval_jaxpr/jit(_cho_solve)/vmap()/triangular_solve | solution.py:74
  318.0 0.6 fusion.71
  318.6 0.6 convolution_subtract_fusion.7
  319.2 0.6 fusion.72
  319.8 0.6 fusion.73
  320.4 0.6 convolution_subtract_fusion.8
  321.1 0.6 convolution_convert_fusion.2
  321.9 1.0 copy-done
  323.0 1.0 copy-done.1
  323.9 0.6 dynamic_slice.33
  326.4 46.9 %custom-call.42 = f32[4,128,128]{2,1,0:T(8,128)S(1)} custom-call(f32[4,128,128]{2,1,0:T(8,128)S(1)} %cholesky.172), custom_call_target="Cholesky" | custom-call | tf_op jit(solution)/shard_map/while/body/eval_jaxpr/jit(cholesky)/cholesky | solution.py:71
  373.4 39.3 %custom-call.43 = f32[4,1,128,128]{2,3,1,0:T(8,128)S(1)} custom-call(f32[4,1,128,128]{3,2,1,0:T(8,128)S(1)} %select_bitcast_fusion.3), custom_call_target="InvertDiagBlocksLowerTriangular" | custom-call | tf_op jit(solution)/shard_map/while/body/eval_jaxpr/jit(cholesky)/cholesky | solution.py:71
  413.1 0.7 convolution_subtract_fusion.6
  413.8 46.9 %custom-call.44 = f32[4,128,128]{2,1,0:T(8,128)S(1)} custom-call(f32[4,128,128]{2,1,0:T(8,128)S(1)} %convolution_subtract_fusion.6), custom_call_target="Cholesky" | custom-call | tf_op jit(solution)/shard_map/while/body/eval_jaxpr/jit(cholesky)/cholesky | solution.py:71
  461.4 3.9 while.18
  461.4 0.6 fusion.74
  462.0 1.3 bitcast_dynamic-update-slice_fusion.5
  463.3 0.6 fusion.74
  463.9 1.3 bitcast_dynamic-update-slice_fusion.5
  465.3 78.6 %custom-call.46 = f32[4,2,128,128]{2,3,1,0:T(8,128)S(1)} custom-call(f32[4,2,128,128]{3,2,1,0:T(8,128)S(1)} %bitcast.144), custom_call_target="InvertDiagBlocksLowerTriangular" | custom-call | tf_op jit(solution)/shard_map/while/body/eval_jaxpr/jit(_cho_solve)/vmap()/triangular_solve | solution.py:74
  544.2 0.6 fusion.71
  544.9 0.6 convolution_subtract_fusion.7
  545.5 0.6 fusion.72
  546.1 0.6 fusion.73
  546.7 0.6 convolution_subtract_fusion.8
  547.4 0.6 convolution_convert_fusion.2
  548.2 1.0 copy-done
  549.2 1.0 copy-done.1
  (116 shorter events, 18.2 us)
Async XLA Ops:
  0.1 8.9 %copy-start.2 = (s32[16]{0:T(128)S(1)}, s32[16]{0:T(128)}, u32[]{:S(2)}) copy-start(s32[16]{0:T(128)} %param.7) | copy-start | bytes 196
  42.5 21.4 %copy-start.3 = (s32[1,16]{1,0:T(1,128)S(1)}, s32[1,16]{1,0:T(1,128)}, u32[]{:S(2)}) copy-start(s32[1,16]{1,0:T(1,128)} %param.6) | copy-start | bytes 196
  44.3 33.2 %all-to-all-start = ((bf16[64,2,512]{2,1,0:T(2,128)(2,1)}), bf16[64,2,512]{2,1,0:T(2,128)(2,1)S(1)}, u32[]{:S(2)}, u32[]{:S(2)}) async-start(bf16[64,2,512]{2,1,0:T(2,128)(2,1)} %reshape.166), calls=%async_computation | async-start | bytes 262144 | tf_op jit(solution)/shard_map/all_to_all | solution.py:44
  321.7 1.2 copy-start
  323.0 1.0 copy-start.1
  548.0 1.2 copy-start
  549.2 1.0 copy-start.1
where the time goes:
time: 552 us; the launch traced here: 550 us
  other arithmetic  435 us (79%)
  local copies, waits for them, and re-layouts  52.2 us (9%)
  starting transfers between devices  19.6 us (4%)
  blocking collectives  16.7 us (3%)
  waiting for transfers between devices  13.6 us (2%)
  matrix products  11.5 us (2%)
    another operation x20, other arithmetic, solve_group(): jnp.linalg.cholesky(auto_part + ridge_term[:, None, None] * jnp.eye(real_...  267 us
    another operation x8, other arithmetic, solve_group(): transfer_t = jax.scipy.linalg.cho_solve((factor, True), cross_part)  158 us
    gather x48, local copies, waits for them, and re-layouts  32.2 us
    all_to_all x1, starting transfers between devices, local(): lax.all_to_all(spectra, 'bin', split_axis=1, concat_axis=4, tiled=True)  19.6 us
    all_gather x1, blocking collectives, local(): references = lax.all_gather(local_refs, 'grp', axis=3, tiled=True)  16.7 us
    all_to_all x1, waiting for transfers between devices, local(): lax.all_to_all(spectra, 'bin', split_axis=1, concat_axis=4, tiled=True)  13.6 us
  transfers between devices with their start and end apart: 1, of which 1 were waited for; matrix products, arithmetic and copies ran while one was open for 0% of the time, Pallas kernels for 0%

commit v1 on v0

v1 whole, which is shorter than its diff:
```python
import math

import jax
import jax.numpy as jnp
import ml_dtypes
import numpy as np
from jax import lax
from jax.experimental import pallas as pl
from jax.experimental.pallas import tpu as pltpu
from jax.sharding import PartitionSpec as P

L = 1024
NB = 512
SEGS = 16
CH = 4
BINS = 8
REFS = 16
LANES = 128
TILES = 8704 // LANES
WINDOW = L + LANES
RIDGE = 0.5

F32 = jnp.float32
BF16 = jnp.bfloat16
MESH = pl.DeviceIdType.MESH


def make_table(bin_devices):
    n = np.arange(L)
    angles = (n[:, None] * np.arange(NB)[None, :] % L).astype(np.float32)
    angles = angles * np.float32(2.0 * math.pi / L)
    hann = np.float32(0.5) - np.float32(0.5) * np.cos(
        n.astype(np.float32) * np.float32(2.0 * math.pi / L)
    )
    parts = np.stack([hann[:, None] * np.cos(angles), -(hann[:, None] * np.sin(angles))])
    parts = parts.reshape(2, L, bin_devices, 2, 4)
    return parts.transpose(4, 0, 2, 3, 1).reshape(2 * NB, L).astype(ml_dtypes.bfloat16)


def nt_dot(a, b):
    return lax.dot_general(a, b, (((1,), (1,)), ((), ())), preferred_element_type=F32)


def tn_dot(a, b):
    return lax.dot_general(a, b, (((0,), (0,)), ((), ())), preferred_element_type=F32)


def cut_segments(offsets, record, segs):
    for s in range(SEGS):
        tile = jnp.minimum(lax.div(offsets[s], LANES), TILES - WINDOW // LANES)
        start = pl.multiple_of(tile * LANES, LANES)
        window = record[0, :, pl.ds(start, WINDOW)].astype(F32)
        window = jnp.concatenate([window, window], axis=0)
        back = lax.rem(WINDOW - (offsets[s] - start), WINDOW)
        cut = pltpu.roll(window, back, axis=1)
        for t in range(L // LANES):
            segs[t, pl.ds(s, CH, stride=SEGS), :] = cut[:CH, t * LANES : (t + 1) * LANES]


def pack_spectra(segs, table, stage, send):
    rows = jnp.concatenate([segs[t] for t in range(L // LANES)], axis=1).astype(BF16)
    rows = jnp.concatenate([rows, rows], axis=0)
    blocks = [nt_dot(table[pl.ds(g * LANES, LANES), :], rows) for g in range(8)]
    group = lax.broadcasted_iota(jnp.int32, (LANES, LANES), 1) // SEGS
    turned = []
    for r in range(4):
        mixed = blocks[r]
        for q in range(1, 8):
            mixed = jnp.where(group == q, blocks[(q + r) % 8], mixed)
        turned.append(pltpu.roll(mixed, SEGS * r, axis=1) if r else mixed)
    phase = lax.rem(group, 4)
    for c in range(CH):
        out = turned[(0 - c) % 4]
        for g in range(1, 4):
            out = jnp.where(phase == g, turned[(g - c) % 4], out)
        stage[pl.ds(c, LANES, stride=CH), :] = out
    send[...] = stage[...].reshape(send.shape).astype(BF16)


def pick_references(ref_index, recv):
    shape = (2 * REFS, recv.shape[0] * BINS)
    row = lax.broadcasted_iota(jnp.int32, shape, 0)
    col = lax.broadcasted_iota(jnp.int32, shape, 1)
    wanted = jnp.full((2 * REFS, 1), -1, jnp.int32)
    slot = lax.broadcasted_iota(jnp.int32, (2 * REFS, 1), 0)
    for i in range(REFS):
        wanted = jnp.where(lax.rem(slot, REFS) == i, ref_index[0, i], wanted)
    place = (wanted // CH) * BINS + lax.rem(wanted, CH) + (row // REFS) * CH
    chosen = jnp.where(col == place, 1.0, 0.0).astype(BF16)
    rows = recv[...].astype(F32).reshape(shape[1], LANES).astype(BF16)
    return jnp.dot(chosen, rows, preferred_element_type=F32).astype(BF16)


def cut_kernel(offsets_hbm, record_hbm, segs, offsets, record, sems):
    load_offsets = pltpu.make_async_copy(offsets_hbm, offsets, sems.at[0])
    load_record = pltpu.make_async_copy(record_hbm, record, sems.at[1])
    load_offsets.start()
    load_record.start()
    load_offsets.wait()
    load_record.wait()
    cut_segments(offsets, record, segs)


def exchange_kernel(ref_index_hbm, segs, table, recv, refs, ref_index, stage, send, sems):
    bins, grps = lax.axis_size("bin"), lax.axis_size("grp")
    me, grp = lax.axis_index("bin"), lax.axis_index("grp")
    load = pltpu.make_async_copy(ref_index_hbm, ref_index, sems.at[0])
    load.start()
    barrier = pltpu.get_barrier_semaphore()

    @pl.loop(1, bins)
    def _(k):
        peer = lax.rem(me + k, bins)
        pl.semaphore_signal(barrier, 1, device_id={"bin": peer}, device_id_type=MESH)

    @pl.loop(1, grps)
    def _(k):
        peer = lax.rem(grp + k, grps)
        pl.semaphore_signal(barrier, 1, device_id={"grp": peer}, device_id_type=MESH)

    pack_spectra(segs, table, stage, send)
    pl.semaphore_wait(barrier, bins + grps - 2)

    @pl.loop(1, bins)
    def _(k):
        peer = lax.rem(me + k, bins)
        pltpu.make_async_remote_copy(
            src_ref=send.at[peer],
            dst_ref=recv.at[me],
            send_sem=sems.at[1],
            recv_sem=sems.at[2],
            device_id={"bin": peer},
            device_id_type=MESH,
        ).start()

    recv[pl.ds(me, 1)] = send[pl.ds(me, 1)]
    load.wait()
    others = recv.at[pl.ds(0, bins - 1)]
    pltpu.make_async_copy(others, others, sems.at[2]).wait()
    refs[pl.ds(grp, 1)] = pick_references(ref_index, recv).reshape(1, 2, REFS, LANES)

    @pl.loop(1, grps)
    def _(k):
        peer = lax.rem(grp + k, grps)
        pltpu.make_async_remote_copy(
            src_ref=refs.at[grp],
            dst_ref=refs.at[grp],
            send_sem=sems.at[3],
            recv_sem=sems.at[4],
            device_id={"grp": peer},
            device_id_type=MESH,
        ).start()

    sent = send.at[pl.ds(0, bins - 1)]
    pltpu.make_async_copy(sent, sent, sems.at[1]).wait()
    other_refs = refs.at[pl.ds(0, grps - 1)]
    pltpu.make_async_copy(other_refs, other_refs, sems.at[4]).wait()
    pltpu.make_async_copy(other_refs, other_refs, sems.at[3]).wait()


def turn(x, imag):
    back = pltpu.roll(x, LANES - SEGS, axis=1)
    ahead = pltpu.roll(x, SEGS, axis=1)
    return jnp.where(imag, ahead, -back)


def lane_pick(x, index):
    return jnp.take_along_axis(x, index, axis=1, mode="promise_in_bounds")


def invert(z, lane, row):
    imag = lax.rem(lane, 32) >= SEGS
    inner = lax.rem(lane, 32)
    base = lane - inner
    segment = lax.rem(row, SEGS)
    for k in range(SEGS):
        col_re = lane_pick(z, base + k)
        col_im = lane_pick(z, base + (SEGS + k))
        pivot_row = jnp.concatenate(
            [
                jnp.broadcast_to(z[h * SEGS + k : h * SEGS + k + 1], (SEGS, LANES))
                for h in range(2)
            ],
            axis=0,
        )
        pivot = jnp.concatenate(
            [
                jnp.broadcast_to(col_re[h * SEGS + k : h * SEGS + k + 1], (SEGS, LANES))
                for h in range(2)
            ],
            axis=0,
        )
        inverse = 1.0 / pivot
        in_col = lax.rem(lane, SEGS) == k
        unit = jnp.where(inner == k, 1.0, 0.0)
        pivot_row = jnp.where(in_col, unit, pivot_row)
        scaled = pivot_row * inverse
        turned = turn(scaled, imag)
        is_row = segment == k
        col_re = jnp.where(is_row, -1.0, col_re)
        col_im = jnp.where(is_row, 0.0, col_im)
        rest = jnp.where(is_row | in_col, 0.0, z)
        z = rest - col_re * scaled - col_im * turned
    return z


def split(x):
    hi = x.astype(BF16)
    return hi, (x - hi.astype(F32)).astype(BF16)


def solve_kernel(recv, refs, out, flat, chans, result, sems):
    sources = recv.shape[0]
    ranks = refs.shape[0] * REFS
    flat[...] = recv[...].astype(F32).reshape(flat.shape)
    for h in range(2):
        for c in range(CH):
            chans[h, pl.ds(c, sources, stride=CH), :] = flat[
                pl.ds(h * CH + c, sources, stride=BINS), :
            ]

    lane = lax.broadcasted_iota(jnp.int32, (LANES, LANES), 1)
    row = lax.broadcasted_iota(jnp.int32, (LANES, LANES), 0)
    same = (lane // 32) == (row // 32)
    lane32, row32 = lane[:32], row[:32]
    inner32 = lax.rem(lane32, 32)
    blocks, grams, ridges = [], [], []
    for h in range(2):
        x = refs[:, h].reshape(ranks, LANES).astype(F32)
        imag = lax.rem(lax.broadcasted_iota(jnp.int32, x.shape, 1), 32) >= SEGS
        block = jnp.concatenate([x, turn(x, imag)], axis=0).astype(BF16)
        blocks.append(block)
        gram = jnp.where(same, tn_dot(block, block), 0.0)
        gram = gram[0:32] + gram[32:64] + gram[64:96] + gram[96:128]
        diagonal = jnp.where(inner32 == row32, gram, 0.0)
        diagonal = jnp.sum(diagonal, axis=0, keepdims=True)
        group_ones = jnp.where(same, 1.0, 0.0)
        trace = jnp.dot(
            jnp.broadcast_to(diagonal, (8, LANES)),
            group_ones,
            precision=lax.Precision.HIGHEST,
            preferred_element_type=F32,
        )
        ridge = (RIDGE / (2 * ranks)) * trace[:1]
        grams.append(gram[:SEGS] + jnp.where(inner32[:SEGS] == row32[:SEGS], ridge, 0.0))

    inverses = invert(jnp.concatenate(grams, axis=0), lane32, row32)
    imag16 = lax.rem(lane[:SEGS], 32) >= SEGS
    copies = []
    for h in range(2):
        upper = inverses[h * SEGS : (h + 1) * SEGS]
        full = jnp.concatenate([upper, turn(upper, imag16)], axis=0)
        full = jnp.where(same, jnp.concatenate([full] * 4, axis=0), 0.0)
        hi, lo = split(full)
        solved = nt_dot(hi, blocks[h]) + nt_dot(lo, blocks[h])
        y = chans[h].astype(BF16)
        y = jnp.concatenate([y, y], axis=1)
        owner = lax.broadcasted_iota(jnp.int32, solved.shape, 0) // 32
        for b in range(4):
            hi, lo = split(jnp.where(owner == b, solved, 0.0))
            weights = jnp.concatenate([hi, lo], axis=0)
            f = h * 4 + b
            result[f] = jnp.dot(y, weights, preferred_element_type=F32).astype(BF16)
            copy = pltpu.make_async_copy(result.at[f], out.at[f], sems.at[f])
            copy.start()
            copies.append(copy)
    for copy in copies:
        copy.wait()


def cut(record, offsets):
    hbm = pl.BlockSpec(memory_space=pltpu.HBM)
    return pl.pallas_call(
        cut_kernel,
        out_shape=jax.ShapeDtypeStruct((L // LANES, CH * SEGS, LANES), F32),
        in_specs=[hbm, hbm],
        out_specs=pl.BlockSpec(memory_space=pltpu.VMEM),
        scratch_shapes=[
            pltpu.SMEM(offsets.shape, jnp.int32),
            pltpu.VMEM(record.shape, BF16),
            pltpu.SemaphoreType.DMA((2,)),
        ],
        compiler_params=pltpu.CompilerParams(vmem_limit_bytes=16 << 20),
        cost_estimate=pl.CostEstimate(flops=0, transcendentals=0, bytes_accessed=6 << 20),
    )(offsets, record)


def exchange(segs, ref_index, table):
    bins, grps = lax.axis_size("bin"), lax.axis_size("grp")
    vmem = pl.BlockSpec(memory_space=pltpu.VMEM)
    return pl.pallas_call(
        exchange_kernel,
        out_shape=(
            jax.ShapeDtypeStruct((bins, BINS, LANES), BF16),
            jax.ShapeDtypeStruct((grps, 2, REFS, LANES), BF16),
        ),
        in_specs=[pl.BlockSpec(memory_space=pltpu.HBM), vmem, vmem],
        out_specs=(vmem, vmem),
        scratch_shapes=[
            pltpu.SMEM(ref_index.shape, jnp.int32),
            pltpu.VMEM((2 * CH * bins, LANES), F32),
            pltpu.VMEM((bins, BINS, LANES), BF16),
            pltpu.SemaphoreType.DMA((5,)),
        ],
        compiler_params=pltpu.CompilerParams(
            collective_id=0, has_side_effects=True, vmem_limit_bytes=16 << 20
        ),
    )(ref_index, segs, table)


def solve(recv, refs):
    sources = recv.shape[0]
    chans = sources * CH
    vmem = pl.BlockSpec(memory_space=pltpu.VMEM)
    width = 2 * refs.shape[0] * REFS
    return pl.pallas_call(
        solve_kernel,
        out_shape=jax.ShapeDtypeStruct((BINS, chans, width), BF16),
        in_specs=[vmem, vmem],
        out_specs=pl.BlockSpec(memory_space=pl.ANY),
        scratch_shapes=[
            pltpu.VMEM((sources * BINS, LANES), F32),
            pltpu.VMEM((2, chans, LANES), F32),
            pltpu.VMEM((BINS, chans, width), BF16),
            pltpu.SemaphoreType.DMA((BINS,)),
        ],
        compiler_params=pltpu.CompilerParams(vmem_limit_bytes=16 << 20),
    )(recv, refs)


def local(record, ref_index, offsets):
    table = jnp.asarray(make_table(lax.axis_size("bin")))
    recv, refs = exchange(cut(record, offsets), ref_index, table)
    return solve(recv, refs)


def solution(mesh):
    placed = (P("grp", "bin", None), P("grp", None), P())
    return jax.shard_map(
        local, mesh=mesh, in_specs=placed, out_specs=P("bin", "grp", None), check_vma=False
    )
```

time: 552 us -> 39.8 us (0.07)
  other arithmetic: 435 us -> 0 us
  local copies, waits for them, and re-layouts: 52.2 us -> 3.78 us
  Pallas kernels: 0 us -> 35.8 us
  starting transfers between devices: 19.6 us -> 0 us
  blocking collectives: 16.7 us -> 0 us
  waiting for transfers between devices: 13.6 us -> 0 us
  matrix products: 11.5 us -> 0 us
    another operation x31 -> x0, other arithmetic: 434 us -> none  [the longest x20 267 us: solve_group(): jnp.linalg.cholesky(auto_part + ridge_term[:, None, None] * jnp.eye(real_...]
    pallas_call x0 -> x3, Pallas kernels: none -> 35.8 us  [the longest x1 30.1 us: exchange(): pl.pallas_call(exchange_kernel, out_shape=(jax.ShapeDtypeStruct((bins, BI...]
    gather x49 -> x0, local copies, waits for them, and re-layouts: 32.8 us -> none
    all_to_all x1 -> x0, starting transfers between devices: 19.6 us -> none  [local(): lax.all_to_all(spectra, 'bin', split_axis=1, concat_axis=4, tiled=True)]
    all_gather x1 -> x0, blocking collectives: 16.7 us -> none  [local(): references = lax.all_gather(local_refs, 'grp', axis=3, tiled=True)]
    all_to_all x1 -> x0, waiting for transfers between devices: 13.6 us -> none  [local(): lax.all_to_all(spectra, 'bin', split_axis=1, concat_axis=4, tiled=True)]
    another operation x16 -> x0, matrix products: 9.44 us -> none  [the longest x12 7.34 us: solve_group(): transfer_t = jax.scipy.linalg.cho_solve((factor, True), cross_part)]
    another operation x18 -> x0, local copies, waits for them, and re-layouts: 8.06 us -> none
  transfers between devices with their start and end apart: 1 -> 0, of which waited for: 1 -> 0; matrix products, arithmetic and copies ran while one was open for 0% -> 0% of each run, Pallas kernels for 0% -> 0%
where the time goes in v1:
time: 39.8 us; the launch traced here: 39.6 us
  Pallas kernels  35.8 us (90%)
  local copies, waits for them, and re-layouts  3.78 us (9%)
    pallas_call x1, Pallas kernels, exchange(): pl.pallas_call(exchange_kernel, out_shape=(jax.ShapeDtypeStruct((bins, BI...  30.1 us
    pallas_call x1, Pallas kernels, solve(): pl.pallas_call(solve_kernel, out_shape=jax.ShapeDtypeStruct((BINS, chans,...  4.81 us
    unnamed x8, local copies, waits for them, and re-layouts  3.78 us
    pallas_call x1, Pallas kernels, cut(): pl.pallas_call(cut_kernel, out_shape=jax.ShapeDtypeStruct((L // LANES, CH...  0.84 us

profile of v1, /device:TPU:1, one launch (start us, length us, event | category | flops | bytes accessed | tf_op | source)
XLA Modules:
  0.0 39.6 jit_solution(5962898931981036197)
XLA Ops:
  0.0 0.0 copy-start.1
  0.0 0.9 %copy-done.1 = bf16[1,4,8704]{2,1,0:T(4,128)(2,1)S(1)} copy-done((bf16[1,4,8704]{2,1,0:T(4,128)(2,1)S(1)}, bf16[1,4,8704]{2,1,0:T(4,128)(2,1)}, u32[]{:S(2)}) %copy-start.1) | copy-done | bytes 69656
  0.9 0.0 copy-start.2
  0.9 0.7 %copy-done.2 = s32[16]{0:T(128)S(1)} copy-done((s32[16]{0:T(128)S(1)}, s32[16]{0:T(128)}, u32[]{:S(2)}) %copy-start.2) | copy-done | bytes 88
  1.5 0.8 %shard_map.46.segs = f32[8,64,128]{2,1,0:T(8,128)S(1)} custom-call(s32[16]{0:T(128)S(1)} %copy-done.2, bf16[1,4,8704]{2,1,0:T(4,128)(2,1)S(1)} %copy-done.1), custom_call_target="tpu_custom_call" | custom-call | bytes 6291456 | tf_op jit(solution)/shard_map/pallas_call | solution.py:273
  2.4 0.0 copy-start
  2.4 1.6 %copy-done = bf16[1024,1024]{1,0:T(8,128)(2,1)S(1)} copy-done((bf16[1024,1024]{1,0:T(8,128)(2,1)S(1)}, bf16[1024,1024]{1,0:T(8,128)(2,1)}, u32[]{:S(2)}) %copy-start) | copy-done | bytes 2097176
  4.0 0.0 copy-start.3
  4.0 0.7 %copy-done.3 = s32[1,16]{1,0:T(1,128)S(1)} copy-done((s32[1,16]{1,0:T(1,128)S(1)}, s32[1,16]{1,0:T(1,128)}, u32[]{:S(2)}) %copy-start.3) | copy-done | bytes 88
  4.6 30.1 %shard_map.47 = (bf16[64,8,128]{2,1,0:T(8,128)(2,1)S(1)}, bf16[8,2,16,128]{3,2,1,0:T(8,128)(2,1)S(1)}) custom-call(s32[1,16]{1,0:T(1,128)S(1)} %copy-done.3, f32[8,64,128]{2,1,0:T(8,128)S(1)} %shard_map.46.segs, bf16[1024,1024]{1,0:T(8,128)(2,1)S(1)} %copy-done), custom_call_target="tpu_custom_call" | custom-call | tf_op jit(solution)/shard_map/pallas_call | solution.py:291
  34.8 4.8 %shard_map.48 = bf16[8,256,256]{2,1,0:T(8,128)(2,1)} custom-call(bf16[64,8,128]{2,1,0:T(8,128)(2,1)S(1)} %get-tuple-element.7.recv, bf16[8,2,16,128]{3,2,1,0:T(8,128)(2,1)S(1)} %get-tuple-element.8.refs), custom_call_target="tpu_custom_call" | custom-call | tf_op jit(solution)/shard_map/pallas_call | solution.py:316
Async XLA Ops:
  0.0 0.9 %copy-start.1 = (bf16[1,4,8704]{2,1,0:T(4,128)(2,1)S(1)}, bf16[1,4,8704]{2,1,0:T(4,128)(2,1)}, u32[]{:S(2)}) copy-start(bf16[1,4,8704]{2,1,0:T(4,128)(2,1)} %record_hbm.1) | copy-start | bytes 208900
  0.9 0.7 %copy-start.2 = (s32[16]{0:T(128)S(1)}, s32[16]{0:T(128)}, u32[]{:S(2)}) copy-start(s32[16]{0:T(128)} %offsets_hbm.1) | copy-start | bytes 196
  2.4 1.6 %copy-start = (bf16[1024,1024]{1,0:T(8,128)(2,1)S(1)}, bf16[1024,1024]{1,0:T(8,128)(2,1)}, u32[]{:S(2)}) copy-start(bf16[1024,1024]{1,0:T(8,128)(2,1)} %constant.2.clone.table) | copy-start | bytes 6291460
  4.0 0.7 %copy-start.3 = (s32[1,16]{1,0:T(1,128)S(1)}, s32[1,16]{1,0:T(1,128)}, u32[]{:S(2)}) copy-start(s32[1,16]{1,0:T(1,128)} %ref_index_hbm.1) | copy-start | bytes 196

commit v2 on v1

--- a/solution.py
+++ b/solution.py
@@ -19,6 +19,7 @@
 TILES = 8704 // LANES
 WINDOW = L + LANES
 RIDGE = 0.5
+VMEM_LIMIT = 16 << 20
 
 F32 = jnp.float32
 BF16 = jnp.bfloat16
@@ -34,7 +35,7 @@
     )
     parts = np.stack([hann[:, None] * np.cos(angles), -(hann[:, None] * np.sin(angles))])
     parts = parts.reshape(2, L, bin_devices, 2, 4)
-    return parts.transpose(4, 0, 2, 3, 1).reshape(2 * NB, L).astype(ml_dtypes.bfloat16)
+    return parts.transpose(4, 0, 2, 3, 1).reshape(8, LANES, L).astype(ml_dtypes.bfloat16)
 
 
 def nt_dot(a, b):
@@ -57,10 +58,13 @@
             segs[t, pl.ds(s, CH, stride=SEGS), :] = cut[:CH, t * LANES : (t + 1) * LANES]
 
 
-def pack_spectra(segs, table, stage, send):
+def pack_spectra(segs, table, loads, stage, send):
     rows = jnp.concatenate([segs[t] for t in range(L // LANES)], axis=1).astype(BF16)
     rows = jnp.concatenate([rows, rows], axis=0)
-    blocks = [nt_dot(table[pl.ds(g * LANES, LANES), :], rows) for g in range(8)]
+    blocks = []
+    for g in range(8):
+        loads[g].wait()
+        blocks.append(nt_dot(table[g], rows))
     group = lax.broadcasted_iota(jnp.int32, (LANES, LANES), 1) // SEGS
     turned = []
     for r in range(4):
@@ -91,39 +95,43 @@
     return jnp.dot(chosen, rows, preferred_element_type=F32).astype(BF16)
 
 
-def cut_kernel(offsets_hbm, record_hbm, segs, offsets, record, sems):
+def spectra_kernel(
+    offsets_hbm, record_hbm, table_hbm, send, offsets, record, table, segs, stage, sems, table_sems
+):
     load_offsets = pltpu.make_async_copy(offsets_hbm, offsets, sems.at[0])
     load_record = pltpu.make_async_copy(record_hbm, record, sems.at[1])
-    load_offsets.start()
-    load_record.start()
+    loads = [
+        pltpu.make_async_copy(table_hbm.at[g], table.at[g], table_sems.at[g]) for g in range(8)
+    ]
+    for load in (load_record, load_offsets, *loads):
+        load.start()
     load_offsets.wait()
     load_record.wait()
     cut_segments(offsets, record, segs)
-
-
-def exchange_kernel(ref_index_hbm, segs, table, recv, refs, ref_index, stage, send, sems):
+    pack_spectra(segs, table, loads, stage, send)
+
+
+def exchange_kernel(ref_index_hbm, send, recv, refs, ref_index, sems, bin_in, grp_in):
     bins, grps = lax.axis_size("bin"), lax.axis_size("grp")
     me, grp = lax.axis_index("bin"), lax.axis_index("grp")
-    load = pltpu.make_async_copy(ref_index_hbm, ref_index, sems.at[0])
-    load.start()
+    load_refs = pltpu.make_async_copy(ref_index_hbm, ref_index, sems.at[0])
+    load_refs.start()
+
     barrier = pltpu.get_barrier_semaphore()
 
-    @pl.loop(1, bins)
-    def _(k):
-        peer = lax.rem(me + k, bins)
+    @pl.loop(me + 1, bins)
+    def _(peer):
         pl.semaphore_signal(barrier, 1, device_id={"bin": peer}, device_id_type=MESH)
 
-    @pl.loop(1, grps)
-    def _(k):
-        peer = lax.rem(grp + k, grps)
+    @pl.loop(grp + 1, grps)
+    def _(peer):
         pl.semaphore_signal(barrier, 1, device_id={"grp": peer}, device_id_type=MESH)
 
-    pack_spectra(segs, table, stage, send)
-    pl.semaphore_wait(barrier, bins + grps - 2)
-
-    @pl.loop(1, bins)
-    def _(k):
-        peer = lax.rem(me + k, bins)
+    @pl.when(me + grp > 0)
+    def _():
+        pl.semaphore_wait(barrier, me + grp)
+
+    def send_to(peer):
         pltpu.make_async_remote_copy(
             src_ref=send.at[peer],
             dst_ref=recv.at[me],
@@ -133,8 +141,34 @@
             device_id_type=MESH,
         ).start()
 
+    @pl.loop(0, me)
+    def _(peer):
+        send_to(peer)
+
+    @pl.loop(0, me)
+    def _(peer):
+        pl.semaphore_signal(
+            bin_in.at[me], 1, device_id={"bin": peer}, device_id_type=MESH
+        )
+
+    @pl.loop(0, grp)
+    def _(peer):
+        pl.semaphore_signal(
+            grp_in.at[grp], 1, device_id={"grp": peer}, device_id_type=MESH
+        )
+
     recv[pl.ds(me, 1)] = send[pl.ds(me, 1)]
-    load.wait()
+
+    @pl.loop(me + 1, bins)
+    def _(peer):
+        pl.semaphore_wait(bin_in.at[peer], 1)
+        send_to(peer)
+
+    @pl.loop(grp + 1, grps)
+    def _(peer):
+        pl.semaphore_wait(grp_in.at[peer], 1)
+
+    load_refs.wait()
     others = recv.at[pl.ds(0, bins - 1)]
     pltpu.make_async_copy(others, others, sems.at[2]).wait()
     refs[pl.ds(grp, 1)] = pick_references(ref_index, recv).reshape(1, 2, REFS, LANES)
@@ -268,24 +302,32 @@
         copy.wait()
 
 
-def cut(record, offsets):
+def in_hbm(x):
+    return pltpu.with_memory_space_constraint(x, pltpu.HBM)
+
+
+def spectra(record, offsets, table):
     hbm = pl.BlockSpec(memory_space=pltpu.HBM)
+    bins = lax.axis_size("bin")
     return pl.pallas_call(
-        cut_kernel,
-        out_shape=jax.ShapeDtypeStruct((L // LANES, CH * SEGS, LANES), F32),
-        in_specs=[hbm, hbm],
+        spectra_kernel,
+        out_shape=jax.ShapeDtypeStruct((bins, BINS, LANES), BF16),
+        in_specs=[hbm, hbm, hbm],
         out_specs=pl.BlockSpec(memory_space=pltpu.VMEM),
         scratch_shapes=[
             pltpu.SMEM(offsets.shape, jnp.int32),
             pltpu.VMEM(record.shape, BF16),
+            pltpu.VMEM(table.shape, BF16),
+            pltpu.VMEM((L // LANES, CH * SEGS, LANES), F32),
+            pltpu.VMEM((2 * CH * bins, LANES), F32),
             pltpu.SemaphoreType.DMA((2,)),
+            pltpu.SemaphoreType.DMA((8,)),
         ],
-        compiler_params=pltpu.CompilerParams(vmem_limit_bytes=16 << 20),
-        cost_estimate=pl.CostEstimate(flops=0, transcendentals=0, bytes_accessed=6 << 20),
-    )(offsets, record)
-
-
-def exchange(segs, ref_index, table):
+        compiler_params=pltpu.CompilerParams(vmem_limit_bytes=VMEM_LIMIT),
+    )(*(in_hbm(x) for x in (offsets, record, table)))
+
+
+def exchange(send, ref_index):
     bins, grps = lax.axis_size("bin"), lax.axis_size("grp")
     vmem = pl.BlockSpec(memory_space=pltpu.VMEM)
     return pl.pallas_call(
@@ -294,18 +336,18 @@
             jax.ShapeDtypeStruct((bins, BINS, LANES), BF16),
             jax.ShapeDtypeStruct((grps, 2, REFS, LANES), BF16),
         ),
-        in_specs=[pl.BlockSpec(memory_space=pltpu.HBM), vmem, vmem],
+        in_specs=[pl.BlockSpec(memory_space=pltpu.HBM), vmem],
         out_specs=(vmem, vmem),
         scratch_shapes=[
             pltpu.SMEM(ref_index.shape, jnp.int32),
-            pltpu.VMEM((2 * CH * bins, LANES), F32),
-            pltpu.VMEM((bins, BINS, LANES), BF16),
             pltpu.SemaphoreType.DMA((5,)),
+            pltpu.SemaphoreType.REGULAR((bins,)),
+            pltpu.SemaphoreType.REGULAR((grps,)),
         ],
         compiler_params=pltpu.CompilerParams(
-            collective_id=0, has_side_effects=True, vmem_limit_bytes=16 << 20
+            collective_id=0, has_side_effects=True, vmem_limit_bytes=VMEM_LIMIT
         ),
-    )(ref_index, segs, table)
+    )(in_hbm(ref_index), send)
 
 
 def solve(recv, refs):
@@ -324,13 +366,13 @@
             pltpu.VMEM((BINS, chans, width), BF16),
             pltpu.SemaphoreType.DMA((BINS,)),
         ],
-        compiler_params=pltpu.CompilerParams(vmem_limit_bytes=16 << 20),
+        compiler_params=pltpu.CompilerParams(vmem_limit_bytes=VMEM_LIMIT),
     )(recv, refs)
 
 
 def local(record, ref_index, offsets):
     table = jnp.asarray(make_table(lax.axis_size("bin")))
-    recv, refs = exchange(cut(record, offsets), ref_index, table)
+    recv, refs = exchange(spectra(record, offsets, table), ref_index)
     return solve(recv, refs)
 
 

time: 39.8 us -> 37.5 us (0.942)
  the two profiles are of different devices: /device:TPU:1 before, /device:TPU:449 now
where the time goes in v2:
time: 37.5 us; the launch traced here: 37.4 us
  Pallas kernels  37.4 us (100%)
    pallas_call x1, Pallas kernels, exchange(): pl.pallas_call(exchange_kernel, out_shape=(jax.ShapeDtypeStruct((bins, BI...  28.5 us
    pallas_call x1, Pallas kernels, solve(): pl.pallas_call(solve_kernel, out_shape=jax.ShapeDtypeStruct((BINS, chans,...  4.81 us
    pallas_call x1, Pallas kernels, spectra(): pl.pallas_call(spectra_kernel, out_shape=jax.ShapeDtypeStruct((bins, BINS...  4.08 us

profile of v2, /device:TPU:449, one launch (start us, length us, event | category | flops | bytes accessed | tf_op | source)
XLA Modules:
  0.0 37.4 jit_solution(13837581250268106219)
XLA Ops:
  0.0 4.1 %shard_map.46.send = bf16[64,8,128]{2,1,0:T(8,128)(2,1)S(1)} custom-call(s32[16]{0:T(128)} %offsets_hbm.1, bf16[1,4,8704]{2,1,0:T(4,128)(2,1)} %record_hbm.1, bf16[8,128,1024]{2,1,0:T(8,128)(2,1)} %constant.2.clone.table_hbm), custom_call_target="tpu_custom_call" | custom-call | tf_op jit(solution)/shard_map/pallas_call | solution.py:312
  4.1 28.5 %shard_map.47 = (bf16[64,8,128]{2,1,0:T(8,128)(2,1)S(1)}, bf16[8,2,16,128]{3,2,1,0:T(8,128)(2,1)S(1)}) custom-call(s32[1,16]{1,0:T(1,128)} %ref_index_hbm.1, bf16[64,8,128]{2,1,0:T(8,128)(2,1)S(1)} %shard_map.46.send), custom_call_target="tpu_custom_call" | custom-call | tf_op jit(solution)/shard_map/pallas_call | solution.py:333
  32.6 4.8 %shard_map.48 = bf16[8,256,256]{2,1,0:T(8,128)(2,1)} custom-call(bf16[64,8,128]{2,1,0:T(8,128)(2,1)S(1)} %get-tuple-element.7.recv, bf16[8,2,16,128]{3,2,1,0:T(8,128)(2,1)S(1)} %get-tuple-element.8.refs), custom_call_target="tpu_custom_call" | custom-call | tf_op jit(solution)/shard_map/pallas_call | solution.py:358

commit v3 on v2

--- a/solution.py
+++ b/solution.py
@@ -17,7 +17,7 @@
 REFS = 16
 LANES = 128
 TILES = 8704 // LANES
-WINDOW = L + LANES
+STEPS = L // LANES + 1
 RIDGE = 0.5
 VMEM_LIMIT = 16 << 20
 
@@ -46,20 +46,44 @@
     return lax.dot_general(a, b, (((0,), (0,)), ((), ())), preferred_element_type=F32)
 
 
-def cut_segments(offsets, record, segs):
+def lane_pick(x, index):
+    return jnp.take_along_axis(x, index, axis=1, mode="promise_in_bounds")
+
+
+def cut_segments(offsets, record, tiles):
+    span = tiles.shape[0] // CH
+    for t in range(span):
+        column = jnp.zeros((CH, LANES), F32)
+        if t < TILES:
+            column = record[0, :, t * LANES : (t + 1) * LANES].astype(F32)
+        tiles[pl.ds(t, CH, stride=span), :] = column
+    source = [tiles[pl.ds(c * span, span), :] for c in range(CH)]
+    source = jnp.concatenate(source, axis=1).astype(BF16)
+
+    row = lax.broadcasted_iota(jnp.int32, (SEGS, LANES), 0)
+    lane = lax.broadcasted_iota(jnp.int32, (SEGS, LANES), 1)
+    start = jnp.zeros((SEGS, LANES), jnp.int32)
     for s in range(SEGS):
-        tile = jnp.minimum(lax.div(offsets[s], LANES), TILES - WINDOW // LANES)
-        start = pl.multiple_of(tile * LANES, LANES)
-        window = record[0, :, pl.ds(start, WINDOW)].astype(F32)
-        window = jnp.concatenate([window, window], axis=0)
-        back = lax.rem(WINDOW - (offsets[s] - start), WINDOW)
-        cut = pltpu.roll(window, back, axis=1)
-        for t in range(L // LANES):
-            segs[t, pl.ds(s, CH, stride=SEGS), :] = cut[:CH, t * LANES : (t + 1) * LANES]
-
-
-def pack_spectra(segs, table, loads, stage, send):
-    rows = jnp.concatenate([segs[t] for t in range(L // LANES)], axis=1).astype(BF16)
+        start = jnp.where(row == s, offsets[s], start)
+    first = jnp.minimum(start >> 7, TILES - STEPS)
+    shift = start - first * LANES
+    chosen = jnp.concatenate([(first + t == lane)[:, :span] for t in range(STEPS)], axis=0)
+    chosen = jnp.where(chosen, 1.0, 0.0).astype(BF16)
+    window = jnp.dot(chosen, source, preferred_element_type=F32)
+    window = window.reshape(STEPS, SEGS, CH * LANES)
+    index = (lane + shift) & (LANES - 1)
+    here = lane + shift < LANES
+    rows = []
+    for c in range(CH):
+        turned = [
+            lane_pick(window[t, :, c * LANES : (c + 1) * LANES], index) for t in range(STEPS)
+        ]
+        cut = [jnp.where(here, turned[t], turned[t + 1]) for t in range(STEPS - 1)]
+        rows.append(jnp.concatenate(cut, axis=1))
+    return jnp.concatenate(rows, axis=0).astype(BF16)
+
+
+def pack_spectra(rows, table, loads, stage, send):
     rows = jnp.concatenate([rows, rows], axis=0)
     blocks = []
     for g in range(8):
@@ -95,41 +119,64 @@
     return jnp.dot(chosen, rows, preferred_element_type=F32).astype(BF16)
 
 
-def spectra_kernel(
-    offsets_hbm, record_hbm, table_hbm, send, offsets, record, table, segs, stage, sems, table_sems
+def bin_of(rank):
+    return (rank // 32) * 32 + lax.rem(rank, 16) * 2 + lax.rem(rank // 16, 2)
+
+
+def rank_of(index):
+    return (index // 32) * 32 + lax.rem(index, 2) * 16 + lax.rem(index // 2, 16)
+
+
+def exchange_kernel(
+    offsets_hbm,
+    ref_index_hbm,
+    record_hbm,
+    table_hbm,
+    recv,
+    refs,
+    offsets,
+    ref_index,
+    record,
+    table,
+    tiles,
+    stage,
+    send,
+    sems,
+    table_sems,
+    bin_in,
+    grp_in,
 ):
+    bins, grps = lax.axis_size("bin"), lax.axis_size("grp")
+    me, grp = lax.axis_index("bin"), lax.axis_index("grp")
+    rank = rank_of(me)
     load_offsets = pltpu.make_async_copy(offsets_hbm, offsets, sems.at[0])
-    load_record = pltpu.make_async_copy(record_hbm, record, sems.at[1])
+    load_record = pltpu.make_async_copy(record_hbm, record, sems.at[5])
+    load_refs = pltpu.make_async_copy(ref_index_hbm, ref_index, sems.at[6])
     loads = [
         pltpu.make_async_copy(table_hbm.at[g], table.at[g], table_sems.at[g]) for g in range(8)
     ]
-    for load in (load_record, load_offsets, *loads):
+    for load in (load_record, load_offsets, *loads, load_refs):
         load.start()
-    load_offsets.wait()
-    load_record.wait()
-    cut_segments(offsets, record, segs)
-    pack_spectra(segs, table, loads, stage, send)
-
-
-def exchange_kernel(ref_index_hbm, send, recv, refs, ref_index, sems, bin_in, grp_in):
-    bins, grps = lax.axis_size("bin"), lax.axis_size("grp")
-    me, grp = lax.axis_index("bin"), lax.axis_index("grp")
-    load_refs = pltpu.make_async_copy(ref_index_hbm, ref_index, sems.at[0])
-    load_refs.start()
 
     barrier = pltpu.get_barrier_semaphore()
 
-    @pl.loop(me + 1, bins)
-    def _(peer):
+    @pl.loop(0, bins - 1 - rank)
+    def _(k):
+        peer = bin_of(bins - 1 - k)
         pl.semaphore_signal(barrier, 1, device_id={"bin": peer}, device_id_type=MESH)
 
     @pl.loop(grp + 1, grps)
     def _(peer):
         pl.semaphore_signal(barrier, 1, device_id={"grp": peer}, device_id_type=MESH)
 
-    @pl.when(me + grp > 0)
+    load_offsets.wait()
+    load_record.wait()
+    rows = cut_segments(offsets, record, tiles)
+    pack_spectra(rows, table, loads, stage, send)
+
+    @pl.when(rank + grp > 0)
     def _():
-        pl.semaphore_wait(barrier, me + grp)
+        pl.semaphore_wait(barrier, rank + grp)
 
     def send_to(peer):
         pltpu.make_async_remote_copy(
@@ -141,26 +188,21 @@
             device_id_type=MESH,
         ).start()
 
-    @pl.loop(0, me)
-    def _(peer):
+    @pl.loop(0, rank)
+    def _(k):
+        peer = bin_of(k)
         send_to(peer)
-
-    @pl.loop(0, me)
-    def _(peer):
-        pl.semaphore_signal(
-            bin_in.at[me], 1, device_id={"bin": peer}, device_id_type=MESH
-        )
+        pl.semaphore_signal(bin_in.at[me], 1, device_id={"bin": peer}, device_id_type=MESH)
 
     @pl.loop(0, grp)
     def _(peer):
-        pl.semaphore_signal(
-            grp_in.at[grp], 1, device_id={"grp": peer}, device_id_type=MESH
-        )
+        pl.semaphore_signal(grp_in.at[grp], 1, device_id={"grp": peer}, device_id_type=MESH)
 
     recv[pl.ds(me, 1)] = send[pl.ds(me, 1)]
 
-    @pl.loop(me + 1, bins)
-    def _(peer):
+    @pl.loop(rank + 1, bins)
+    def _(k):
+        peer = bin_of(k)
         pl.semaphore_wait(bin_in.at[peer], 1)
         send_to(peer)
 
@@ -196,10 +238,6 @@
     back = pltpu.roll(x, LANES - SEGS, axis=1)
     ahead = pltpu.roll(x, SEGS, axis=1)
     return jnp.where(imag, ahead, -back)
-
-
-def lane_pick(x, index):
-    return jnp.take_along_axis(x, index, axis=1, mode="promise_in_bounds")
 
 
 def invert(z, lane, row):
@@ -306,48 +344,35 @@
     return pltpu.with_memory_space_constraint(x, pltpu.HBM)
 
 
-def spectra(record, offsets, table):
-    hbm = pl.BlockSpec(memory_space=pltpu.HBM)
-    bins = lax.axis_size("bin")
-    return pl.pallas_call(
-        spectra_kernel,
-        out_shape=jax.ShapeDtypeStruct((bins, BINS, LANES), BF16),
-        in_specs=[hbm, hbm, hbm],
-        out_specs=pl.BlockSpec(memory_space=pltpu.VMEM),
-        scratch_shapes=[
-            pltpu.SMEM(offsets.shape, jnp.int32),
-            pltpu.VMEM(record.shape, BF16),
-            pltpu.VMEM(table.shape, BF16),
-            pltpu.VMEM((L // LANES, CH * SEGS, LANES), F32),
-            pltpu.VMEM((2 * CH * bins, LANES), F32),
-            pltpu.SemaphoreType.DMA((2,)),
-            pltpu.SemaphoreType.DMA((8,)),
-        ],
-        compiler_params=pltpu.CompilerParams(vmem_limit_bytes=VMEM_LIMIT),
-    )(*(in_hbm(x) for x in (offsets, record, table)))
-
-
-def exchange(send, ref_index):
+def exchange(record, ref_index, offsets, table):
     bins, grps = lax.axis_size("bin"), lax.axis_size("grp")
     vmem = pl.BlockSpec(memory_space=pltpu.VMEM)
+    hbm = pl.BlockSpec(memory_space=pltpu.HBM)
     return pl.pallas_call(
         exchange_kernel,
         out_shape=(
             jax.ShapeDtypeStruct((bins, BINS, LANES), BF16),
             jax.ShapeDtypeStruct((grps, 2, REFS, LANES), BF16),
         ),
-        in_specs=[pl.BlockSpec(memory_space=pltpu.HBM), vmem],
+        in_specs=[hbm, hbm, hbm, hbm],
         out_specs=(vmem, vmem),
         scratch_shapes=[
+            pltpu.SMEM(offsets.shape, jnp.int32),
             pltpu.SMEM(ref_index.shape, jnp.int32),
-            pltpu.SemaphoreType.DMA((5,)),
+            pltpu.VMEM(record.shape, BF16),
+            pltpu.VMEM(table.shape, BF16),
+            pltpu.VMEM((CH * 72, LANES), F32),
+            pltpu.VMEM((2 * CH * bins, LANES), F32),
+            pltpu.VMEM((bins, BINS, LANES), BF16),
+            pltpu.SemaphoreType.DMA((7,)),
+            pltpu.SemaphoreType.DMA((8,)),
             pltpu.SemaphoreType.REGULAR((bins,)),
             pltpu.SemaphoreType.REGULAR((grps,)),
         ],
         compiler_params=pltpu.CompilerParams(
             collective_id=0, has_side_effects=True, vmem_limit_bytes=VMEM_LIMIT
         ),
-    )(in_hbm(ref_index), send)
+    )(*(in_hbm(x) for x in (offsets, ref_index, record, table)))
 
 
 def solve(recv, refs):
@@ -372,7 +397,7 @@
 
 def local(record, ref_index, offsets):
     table = jnp.asarray(make_table(lax.axis_size("bin")))
-    recv, refs = exchange(spectra(record, offsets, table), ref_index)
+    recv, refs = exchange(record, ref_index, offsets, table)
     return solve(recv, refs)
 
 

time: 37.5 us -> 35 us (0.933)
  the two profiles are of different devices: /device:TPU:449 before, /device:TPU:1 now
where the time goes in v3:
time: 35 us; the launch traced here: 34.9 us
  Pallas kernels  34.9 us (100%)
    pallas_call x1, Pallas kernels, exchange(): pl.pallas_call(exchange_kernel, out_shape=(jax.ShapeDtypeStruct((bins, BI...  30.1 us
    pallas_call x1, Pallas kernels, solve(): pl.pallas_call(solve_kernel, out_shape=jax.ShapeDtypeStruct((BINS, chans,...  4.81 us

profile of v3, /device:TPU:1, one launch (start us, length us, event | category | flops | bytes accessed | tf_op | source)
XLA Modules:
  0.0 34.9 jit_solution(16587372040256448130)
XLA Ops:
  0.0 30.1 %shard_map.46 = (bf16[64,8,128]{2,1,0:T(8,128)(2,1)S(1)}, bf16[8,2,16,128]{3,2,1,0:T(8,128)(2,1)S(1)}) custom-call(s32[16]{0:T(128)} %offsets_hbm.1, s32[1,16]{1,0:T(1,128)} %ref_index_hbm.1, bf16[1,4,8704]{2,1,0:T(4,128)(2,1)} %record_hbm.1, bf16[8,128,1024]{2,1,0:T(8,128)(2,1)} %constant.2.clone.table_hbm), custom_call_target="tpu_custom_call" | custom-call | tf_op jit(solution)/shard_map/pallas_call | solution.py:351
  30.1 4.8 %shard_map.47 = bf16[8,256,256]{2,1,0:T(8,128)(2,1)} custom-call(bf16[64,8,128]{2,1,0:T(8,128)(2,1)S(1)} %get-tuple-element.7.recv, bf16[8,2,16,128]{3,2,1,0:T(8,128)(2,1)S(1)} %get-tuple-element.8.refs), custom_call_target="tpu_custom_call" | custom-call | tf_op jit(solution)/shard_map/pallas_call | solution.py:383

commit v4 on v3

--- a/solution.py
+++ b/solution.py
@@ -241,38 +241,46 @@
 
 
 def invert(z, lane, row):
-    imag = lax.rem(lane, 32) >= SEGS
     inner = lax.rem(lane, 32)
     base = lane - inner
+    column = lax.rem(lane, SEGS)
     segment = lax.rem(row, SEGS)
-    for k in range(SEGS):
-        col_re = lane_pick(z, base + k)
-        col_im = lane_pick(z, base + (SEGS + k))
-        pivot_row = jnp.concatenate(
-            [
-                jnp.broadcast_to(z[h * SEGS + k : h * SEGS + k + 1], (SEGS, LANES))
-                for h in range(2)
-            ],
-            axis=0,
+    few = slice(0, 2)
+    imag, base2 = inner[few] >= SEGS, base[few]
+
+    def pivot_row(k):
+        return jnp.concatenate([z[k : k + 1], z[SEGS + k : SEGS + k + 1]], axis=0)
+
+    def spread(x):
+        return jnp.concatenate(
+            [jnp.broadcast_to(x[h : h + 1], (SEGS, LANES)) for h in range(2)], axis=0
         )
-        pivot = jnp.concatenate(
-            [
-                jnp.broadcast_to(col_re[h * SEGS + k : h * SEGS + k + 1], (SEGS, LANES))
-                for h in range(2)
-            ],
-            axis=0,
-        )
-        inverse = 1.0 / pivot
-        in_col = lax.rem(lane, SEGS) == k
-        unit = jnp.where(inner == k, 1.0, 0.0)
-        pivot_row = jnp.where(in_col, unit, pivot_row)
-        scaled = pivot_row * inverse
-        turned = turn(scaled, imag)
-        is_row = segment == k
-        col_re = jnp.where(is_row, -1.0, col_re)
-        col_im = jnp.where(is_row, 0.0, col_im)
-        rest = jnp.where(is_row | in_col, 0.0, z)
-        z = rest - col_re * scaled - col_im * turned
+
+    for k in range(0, SEGS, 2):
+        m = k + 1
+        in_cols = (column == k) | (column == m)
+        r0, r1 = pivot_row(k), pivot_row(m)
+        a = lane_pick(r0, base2 + k)
+        b_re = lane_pick(r0, base2 + m)
+        b_im = lane_pick(r0, base2 + (SEGS + m))
+        d = lane_pick(r1, base2 + m)
+        inverse = 1.0 / (a * d - (b_re * b_re + b_im * b_im))
+        a, d, b_re, b_im = a * inverse, d * inverse, b_re * inverse, b_im * inverse
+        e0 = jnp.where(in_cols[few], jnp.where(inner[few] == k, 1.0, 0.0), r0)
+        e1 = jnp.where(in_cols[few], jnp.where(inner[few] == m, 1.0, 0.0), r1)
+        t0, t1 = turn(e0, imag), turn(e1, imag)
+        w0 = spread(d * e0 - b_re * e1 - b_im * t1)
+        w1 = spread(a * e1 - b_re * e0 + b_im * t0)
+        tw0 = spread(d * t0 - b_re * t1 + b_im * e1)
+        tw1 = spread(a * t1 - b_re * t0 - b_im * e0)
+        is0, is1 = segment == k, segment == m
+        is_row = is0 | is1
+        c0_re = jnp.where(is_row, jnp.where(is0, -1.0, 0.0), lane_pick(z, base + k))
+        c0_im = jnp.where(is_row, 0.0, lane_pick(z, base + (SEGS + k)))
+        c1_re = jnp.where(is_row, jnp.where(is1, -1.0, 0.0), lane_pick(z, base + m))
+        c1_im = jnp.where(is_row, 0.0, lane_pick(z, base + (SEGS + m)))
+        rest = jnp.where(is_row | in_cols, 0.0, z)
+        z = rest - (c0_re * w0 + c0_im * tw0) - (c1_re * w1 + c1_im * tw1)
     return z
 
 

time: 35 us -> 33.4 us (0.954)
  Pallas kernels: 34.9 us -> 33.2 us
    pallas_call x1, Pallas kernels: 4.81 us -> 3.14 us  [solve(): pl.pallas_call(solve_kernel, out_shape=jax.ShapeDtypeStruct((BINS, chans,...]
where the time goes in v4:
time: 33.4 us; the launch traced here: 33.3 us
  Pallas kernels  33.2 us (99%)
    pallas_call x1, Pallas kernels, exchange(): pl.pallas_call(exchange_kernel, out_shape=(jax.ShapeDtypeStruct((bins, BI...  30.1 us
    pallas_call x1, Pallas kernels, solve(): pl.pallas_call(solve_kernel, out_shape=jax.ShapeDtypeStruct((BINS, chans,...  3.14 us

profile of v4, /device:TPU:1, one launch (start us, length us, event | category | flops | bytes accessed | tf_op | source)
XLA Modules:
  0.0 33.3 jit_solution(18390364707456949472)
XLA Ops:
  0.0 30.1 %shard_map.46 = (bf16[64,8,128]{2,1,0:T(8,128)(2,1)S(1)}, bf16[8,2,16,128]{3,2,1,0:T(8,128)(2,1)S(1)}) custom-call(s32[16]{0:T(128)} %offsets_hbm.1, s32[1,16]{1,0:T(1,128)} %ref_index_hbm.1, bf16[1,4,8704]{2,1,0:T(4,128)(2,1)} %record_hbm.1, bf16[8,128,1024]{2,1,0:T(8,128)(2,1)} %constant.2.clone.table_hbm), custom_call_target="tpu_custom_call" | custom-call | tf_op jit(solution)/shard_map/pallas_call | solution.py:359
  30.1 3.1 %shard_map.47 = bf16[8,256,256]{2,1,0:T(8,128)(2,1)} custom-call(bf16[64,8,128]{2,1,0:T(8,128)(2,1)S(1)} %get-tuple-element.7.recv, bf16[8,2,16,128]{3,2,1,0:T(8,128)(2,1)S(1)} %get-tuple-element.8.refs), custom_call_target="tpu_custom_call" | custom-call | tf_op jit(solution)/shard_map/pallas_call | solution.py:391

commit v5 on v4

--- a/solution.py
+++ b/solution.py
@@ -119,14 +119,6 @@
     return jnp.dot(chosen, rows, preferred_element_type=F32).astype(BF16)
 
 
-def bin_of(rank):
-    return (rank // 32) * 32 + lax.rem(rank, 16) * 2 + lax.rem(rank // 16, 2)
-
-
-def rank_of(index):
-    return (index // 32) * 32 + lax.rem(index, 2) * 16 + lax.rem(index // 2, 16)
-
-
 def exchange_kernel(
     offsets_hbm,
     ref_index_hbm,
@@ -148,7 +140,11 @@
 ):
     bins, grps = lax.axis_size("bin"), lax.axis_size("grp")
     me, grp = lax.axis_index("bin"), lax.axis_index("grp")
-    rank = rank_of(me)
+    grp_rank = grp + lax.rem(me, 2) * (grps - 1 - 2 * grp)
+
+    def in_grp(k):
+        return {"grp": k + lax.rem(me, 2) * (grps - 1 - 2 * k)}
+
     load_offsets = pltpu.make_async_copy(offsets_hbm, offsets, sems.at[0])
     load_record = pltpu.make_async_copy(record_hbm, record, sems.at[5])
     load_refs = pltpu.make_async_copy(ref_index_hbm, ref_index, sems.at[6])
@@ -160,23 +156,25 @@
 
     barrier = pltpu.get_barrier_semaphore()
 
-    @pl.loop(0, bins - 1 - rank)
+    @pl.loop(0, bins - 1 - me)
     def _(k):
-        peer = bin_of(bins - 1 - k)
+        peer = bins - 1 - k
         pl.semaphore_signal(barrier, 1, device_id={"bin": peer}, device_id_type=MESH)
 
-    @pl.loop(grp + 1, grps)
-    def _(peer):
-        pl.semaphore_signal(barrier, 1, device_id={"grp": peer}, device_id_type=MESH)
+    @pl.loop(grp_rank + 1, grps)
+    def _(k):
+        pl.semaphore_signal(barrier, 1, device_id=in_grp(k), device_id_type=MESH)
 
     load_offsets.wait()
     load_record.wait()
     rows = cut_segments(offsets, record, tiles)
     pack_spectra(rows, table, loads, stage, send)
 
-    @pl.when(rank + grp > 0)
+    before = me + grp_rank
+
+    @pl.when(before > 0)
     def _():
-        pl.semaphore_wait(barrier, rank + grp)
+        pl.semaphore_wait(barrier, before)
 
     def send_to(peer):
         pltpu.make_async_remote_copy(
@@ -188,27 +186,25 @@
             device_id_type=MESH,
         ).start()
 
-    @pl.loop(0, rank)
-    def _(k):
-        peer = bin_of(k)
+    @pl.loop(0, me)
+    def _(peer):
         send_to(peer)
         pl.semaphore_signal(bin_in.at[me], 1, device_id={"bin": peer}, device_id_type=MESH)
 
-    @pl.loop(0, grp)
+    @pl.loop(0, grp_rank)
+    def _(k):
+        pl.semaphore_signal(grp_in.at[grp_rank], 1, device_id=in_grp(k), device_id_type=MESH)
+
+    recv[pl.ds(me, 1)] = send[pl.ds(me, 1)]
+
+    @pl.loop(me + 1, bins)
     def _(peer):
-        pl.semaphore_signal(grp_in.at[grp], 1, device_id={"grp": peer}, device_id_type=MESH)
-
-    recv[pl.ds(me, 1)] = send[pl.ds(me, 1)]
-
-    @pl.loop(rank + 1, bins)
-    def _(k):
-        peer = bin_of(k)
         pl.semaphore_wait(bin_in.at[peer], 1)
         send_to(peer)
 
-    @pl.loop(grp + 1, grps)
-    def _(peer):
-        pl.semaphore_wait(grp_in.at[peer], 1)
+    @pl.loop(grp_rank + 1, grps)
+    def _(k):
+        pl.semaphore_wait(grp_in.at[k], 1)
 
     load_refs.wait()
     others = recv.at[pl.ds(0, bins - 1)]

time: 33.4 us -> 31.3 us (0.937); the launches traced: 33.3 us -> 30.8 us
  Pallas kernels: 33.2 us -> 30.8 us
    pallas_call x1, Pallas kernels: 30.1 us -> 27.6 us  [exchange(): pl.pallas_call(exchange_kernel, out_shape=(jax.ShapeDtypeStruct((bins, BI...]
where the time goes in v5:
time: 31.3 us; the launch traced here: 30.8 us
  Pallas kernels  30.8 us (98%)
    pallas_call x1, Pallas kernels, exchange(): pl.pallas_call(exchange_kernel, out_shape=(jax.ShapeDtypeStruct((bins, BI...  27.6 us
    pallas_call x1, Pallas kernels, solve(): pl.pallas_call(solve_kernel, out_shape=jax.ShapeDtypeStruct((BINS, chans,...  3.14 us

profile of v5, /device:TPU:1, one launch (start us, length us, event | category | flops | bytes accessed | tf_op | source)
XLA Modules:
  0.0 30.8 jit_solution(16753887089576699993)
XLA Ops:
  0.0 27.6 %shard_map.46 = (bf16[64,8,128]{2,1,0:T(8,128)(2,1)S(1)}, bf16[8,2,16,128]{3,2,1,0:T(8,128)(2,1)S(1)}) custom-call(s32[16]{0:T(128)} %offsets_hbm.1, s32[1,16]{1,0:T(1,128)} %ref_index_hbm.1, bf16[1,4,8704]{2,1,0:T(4,128)(2,1)} %record_hbm.1, bf16[8,128,1024]{2,1,0:T(8,128)(2,1)} %constant.2.clone.table_hbm), custom_call_target="tpu_custom_call" | custom-call | tf_op jit(solution)/shard_map/pallas_call | solution.py:355
  27.6 3.1 %shard_map.47 = bf16[8,256,256]{2,1,0:T(8,128)(2,1)} custom-call(bf16[64,8,128]{2,1,0:T(8,128)(2,1)S(1)} %get-tuple-element.7.recv, bf16[8,2,16,128]{3,2,1,0:T(8,128)(2,1)S(1)} %get-tuple-element.8.refs), custom_call_target="tpu_custom_call" | custom-call | tf_op jit(solution)/shard_map/pallas_call | solution.py:387

commit v6 on v5

--- a/solution.py
+++ b/solution.py
@@ -105,8 +105,8 @@
     send[...] = stage[...].reshape(send.shape).astype(BF16)
 
 
-def pick_references(ref_index, recv):
-    shape = (2 * REFS, recv.shape[0] * BINS)
+def reference_choice(ref_index, sources):
+    shape = (2 * REFS, sources * BINS)
     row = lax.broadcasted_iota(jnp.int32, shape, 0)
     col = lax.broadcasted_iota(jnp.int32, shape, 1)
     wanted = jnp.full((2 * REFS, 1), -1, jnp.int32)
@@ -114,9 +114,7 @@
     for i in range(REFS):
         wanted = jnp.where(lax.rem(slot, REFS) == i, ref_index[0, i], wanted)
     place = (wanted // CH) * BINS + lax.rem(wanted, CH) + (row // REFS) * CH
-    chosen = jnp.where(col == place, 1.0, 0.0).astype(BF16)
-    rows = recv[...].astype(F32).reshape(shape[1], LANES).astype(BF16)
-    return jnp.dot(chosen, rows, preferred_element_type=F32).astype(BF16)
+    return jnp.where(col == place, 1.0, 0.0).astype(BF16)
 
 
 def exchange_kernel(
@@ -207,9 +205,12 @@
         pl.semaphore_wait(grp_in.at[k], 1)
 
     load_refs.wait()
+    choice = reference_choice(ref_index, bins)
     others = recv.at[pl.ds(0, bins - 1)]
     pltpu.make_async_copy(others, others, sems.at[2]).wait()
-    refs[pl.ds(grp, 1)] = pick_references(ref_index, recv).reshape(1, 2, REFS, LANES)
+    received = recv[...].astype(F32).reshape(bins * BINS, LANES).astype(BF16)
+    chosen = jnp.dot(choice, received, preferred_element_type=F32).astype(BF16)
+    refs[pl.ds(grp, 1)] = chosen.reshape(1, 2, REFS, LANES)
 
     @pl.loop(1, grps)
     def _(k):
@@ -300,7 +301,8 @@
     same = (lane // 32) == (row // 32)
     lane32, row32 = lane[:32], row[:32]
     inner32 = lax.rem(lane32, 32)
-    blocks, grams, ridges = [], [], []
+    ones = jnp.concatenate([jnp.where(same, 1.0, 0.0).astype(BF16)] * 3, axis=0)
+    blocks, grams = [], []
     for h in range(2):
         x = refs[:, h].reshape(ranks, LANES).astype(F32)
         imag = lax.rem(lax.broadcasted_iota(jnp.int32, x.shape, 1), 32) >= SEGS
@@ -310,13 +312,11 @@
         gram = gram[0:32] + gram[32:64] + gram[64:96] + gram[96:128]
         diagonal = jnp.where(inner32 == row32, gram, 0.0)
         diagonal = jnp.sum(diagonal, axis=0, keepdims=True)
-        group_ones = jnp.where(same, 1.0, 0.0)
-        trace = jnp.dot(
-            jnp.broadcast_to(diagonal, (8, LANES)),
-            group_ones,
-            precision=lax.Precision.HIGHEST,
-            preferred_element_type=F32,
-        )
+        hi, lo = split(diagonal)
+        lost = (diagonal - hi.astype(F32) - lo.astype(F32)).astype(BF16)
+        parts = jnp.concatenate([hi, lo, lost], axis=1)
+        parts = jnp.broadcast_to(parts.astype(F32), (16, 3 * LANES)).astype(BF16)
+        trace = jnp.dot(parts, ones, preferred_element_type=F32)
         ridge = (RIDGE / (2 * ranks)) * trace[:1]
         grams.append(gram[:SEGS] + jnp.where(inner32[:SEGS] == row32[:SEGS], ridge, 0.0))
 

time: 31.3 us -> 31.2 us (level)
  no operation moved by 1% of the time
where the time goes in v6:
time: 31.2 us; the launch traced here: 30.7 us
  Pallas kernels  30.7 us (98%)
    pallas_call x1, Pallas kernels, exchange(): pl.pallas_call(exchange_kernel, out_shape=(jax.ShapeDtypeStruct((bins, BI...  27.6 us
    pallas_call x1, Pallas kernels, solve(): pl.pallas_call(solve_kernel, out_shape=jax.ShapeDtypeStruct((BINS, chans,...  3.07 us

profile of v6, /device:TPU:1, one launch (start us, length us, event | category | flops | bytes accessed | tf_op | source)
XLA Modules:
  0.0 30.7 jit_solution(16015080758708959846)
XLA Ops:
  0.0 27.6 %shard_map.46 = (bf16[64,8,128]{2,1,0:T(8,128)(2,1)S(1)}, bf16[8,2,16,128]{3,2,1,0:T(8,128)(2,1)S(1)}) custom-call(s32[16]{0:T(128)} %offsets_hbm.1, s32[1,16]{1,0:T(1,128)} %ref_index_hbm.1, bf16[1,4,8704]{2,1,0:T(4,128)(2,1)} %record_hbm.1, bf16[8,128,1024]{2,1,0:T(8,128)(2,1)} %constant.2.clone.table_hbm), custom_call_target="tpu_custom_call" | custom-call | tf_op jit(solution)/shard_map/pallas_call | solution.py:355
  27.6 3.1 %shard_map.47 = bf16[8,256,256]{2,1,0:T(8,128)(2,1)} custom-call(bf16[64,8,128]{2,1,0:T(8,128)(2,1)S(1)} %get-tuple-element.7.recv, bf16[8,2,16,128]{3,2,1,0:T(8,128)(2,1)S(1)} %get-tuple-element.8.refs), custom_call_target="tpu_custom_call" | custom-call | tf_op jit(solution)/shard_map/pallas_call | solution.py:387

commit v7 on v5

--- a/solution.py
+++ b/solution.py
@@ -211,17 +211,22 @@
     pltpu.make_async_copy(others, others, sems.at[2]).wait()
     refs[pl.ds(grp, 1)] = pick_references(ref_index, recv).reshape(1, 2, REFS, LANES)
 
-    @pl.loop(1, grps)
+    upper = grp // (grps // 2)
+
+    @pl.loop(0, grps)
     def _(k):
-        peer = lax.rem(grp + k, grps)
-        pltpu.make_async_remote_copy(
-            src_ref=refs.at[grp],
-            dst_ref=refs.at[grp],
-            send_sem=sems.at[3],
-            recv_sem=sems.at[4],
-            device_id={"grp": peer},
-            device_id_type=MESH,
-        ).start()
+        peer = upper * k + (1 - upper) * (grps - 1 - k)
+
+        @pl.when(peer != grp)
+        def _():
+            pltpu.make_async_remote_copy(
+                src_ref=refs.at[grp],
+                dst_ref=refs.at[grp],
+                send_sem=sems.at[3],
+                recv_sem=sems.at[4],
+                device_id={"grp": peer},
+                device_id_type=MESH,
+            ).start()
 
     sent = send.at[pl.ds(0, bins - 1)]
     pltpu.make_async_copy(sent, sent, sems.at[1]).wait()

time: 31.3 us -> 31.3 us (level)
  no operation moved by 1% of the time
where the time goes in v7:
time: 31.3 us; the launch traced here: 30.7 us
  Pallas kernels  30.7 us (98%)
    pallas_call x1, Pallas kernels, exchange(): pl.pallas_call(exchange_kernel, out_shape=(jax.ShapeDtypeStruct((bins, BI...  27.6 us
    pallas_call x1, Pallas kernels, solve(): pl.pallas_call(solve_kernel, out_shape=jax.ShapeDtypeStruct((BINS, chans,...  3.14 us

profile of v7, /device:TPU:1, one launch (start us, length us, event | category | flops | bytes accessed | tf_op | source)
XLA Modules:
  0.0 30.7 jit_solution(17321465094626981586)
XLA Ops:
  0.0 27.6 %shard_map.46 = (bf16[64,8,128]{2,1,0:T(8,128)(2,1)S(1)}, bf16[8,2,16,128]{3,2,1,0:T(8,128)(2,1)S(1)}) custom-call(s32[16]{0:T(128)} %offsets_hbm.1, s32[1,16]{1,0:T(1,128)} %ref_index_hbm.1, bf16[1,4,8704]{2,1,0:T(4,128)(2,1)} %record_hbm.1, bf16[8,128,1024]{2,1,0:T(8,128)(2,1)} %constant.2.clone.table_hbm), custom_call_target="tpu_custom_call" | custom-call | tf_op jit(solution)/shard_map/pallas_call | solution.py:360
  27.6 3.1 %shard_map.47 = bf16[8,256,256]{2,1,0:T(8,128)(2,1)} custom-call(bf16[64,8,128]{2,1,0:T(8,128)(2,1)S(1)} %get-tuple-element.7.recv, bf16[8,2,16,128]{3,2,1,0:T(8,128)(2,1)S(1)} %get-tuple-element.8.refs), custom_call_target="tpu_custom_call" | custom-call | tf_op jit(solution)/shard_map/pallas_call | solution.py:392
